TPU v7x, 512 devices: a whole 4x4x16 slice. The times are simulated.
512 devices in a mesh: ctx: 32 (over x, z_lo, core), tp: 16 (over y, z_hi).
Axes of the slice: x: 4, y: 4, z: 16 (z_hi: 4, z_lo: 4; z = z_hi * 4 + z_lo), core: 2. Of those that a mesh axis runs over, the one named last changes fastest.
Arguments:
- queries: bfloat16 [8192, 4096], P('ctx', 'tp'), may hold values from -6 to 6
- keys: bfloat16 [8192, 512], P('ctx'), may hold values from -6 to 6
- values: bfloat16 [8192, 512], P('ctx'), may hold values from -6 to 6
- out_weight: bfloat16 [4096, 8192], P('tp'), may hold values from -0.125 to 0.125
- storm_mask: int32 [64, 64], replicated, may hold values from 0 to 1, as said below
Outputs:
- mixed: bfloat16 [8192, 8192], P('ctx', 'tp')
Inputs may be any that keep to these rules, and one draw needn't show every extreme that they name: storm_mask[i, j] is 0 where j > i and 1 where 0 <= i - j < 4.
All inputs are finite; a program needn't handle non-finite values.
Results may differ from a plain program's by a relative error of at most 0.019.
Values may be sent and summed in bfloat16 or wider, within the bound.
A program may use at most 64 MiB of HBM per device.

v0:
```python
import jax
import jax.numpy as jnp
from jax import lax
from jax.sharding import PartitionSpec as P

HDIM = 128
BLOCK = 128
GQ = 8


def rows_of_mask(index_of_block, storm_mask):
    blocks = storm_mask.shape[0]
    one_hot = (index_of_block[:, None] == jnp.arange(blocks)[None, :]).astype(jnp.float32)
    return jnp.dot(one_hot, storm_mask.astype(jnp.float32))


def update(carry, query, keys_part, values_part, first, row_mask):
    count = keys_part.shape[0]
    blocks = row_mask.shape[1]
    block_of = (first + jnp.arange(count)) // BLOCK
    one_hot = (jnp.arange(blocks)[:, None] == block_of[None, :]).astype(jnp.float32)
    allowed = jnp.dot(row_mask, one_hot) > 0.5

    def compute(state):
        maximum, total, running_total = state
        scores = jnp.einsum(
            "qhd,kd->hqk", query, keys_part, preferred_element_type=jnp.float32
        ) * HDIM ** (-0.5)
        scores = jnp.where(allowed[None], scores, -1e30)
        peak = jnp.maximum(maximum, jnp.max(scores, axis=2))
        weights = jnp.where(allowed[None], jnp.exp(scores - peak[:, :, None]), 0.0)
        factor = jnp.exp(maximum - peak)
        total = total * factor + jnp.sum(weights, axis=2)
        running_total = running_total * factor[:, :, None] + jnp.einsum(
            "hqk,kd->hqd",
            weights.astype(jnp.bfloat16),
            values_part,
            preferred_element_type=jnp.float32,
        )
        return (peak, total, running_total)

    return lax.cond(jnp.any(allowed), compute, lambda state: state, carry)


def body(queries, keys, values, out_weight, storm_mask):
    rows, width = queries.shape
    heads = width // HDIM
    place = lax.axis_index("ctx")
    shared_head = lax.axis_index("tp") * heads // GQ
    local_keys = lax.dynamic_slice_in_dim(keys, shared_head * HDIM, HDIM, 1)
    own_values = lax.dynamic_slice_in_dim(values, shared_head * HDIM, HDIM, 1)
    per_device = rows // BLOCK
    owned = place * per_device + jnp.arange(per_device)
    row_mask = jnp.repeat(rows_of_mask(owned, storm_mask), BLOCK, axis=0)
    query = queries.reshape(rows, heads, HDIM)
    initial = (
        jnp.full((heads, rows), -1e30, jnp.float32),
        jnp.zeros((heads, rows), jnp.float32),
        jnp.zeros((heads, rows, HDIM), jnp.float32),
    )
    carry = initial
    keys_part = lax.all_gather(local_keys, "ctx", axis=0, tiled=True)
    values_part = lax.all_gather(own_values, "ctx", axis=0, tiled=True)
    count = keys_part.shape[0]
    stride = 512

    def inner(state, number):
        first = number * stride
        keys_block = lax.dynamic_slice_in_dim(keys_part, first, stride, 0)
        values_block = lax.dynamic_slice_in_dim(values_part, first, stride, 0)
        return (update(state, query, keys_block, values_block, first, row_mask), None)

    carry, unused = lax.scan(inner, carry, jnp.arange(count // stride))
    maximum, total, running_total = carry
    attended = (
        (running_total / total[:, :, None])
        .astype(jnp.bfloat16)
        .transpose(1, 0, 2)
        .reshape(rows, width)
    )
    columns = out_weight.shape[1] // lax.axis_size("tp")
    whole = lax.psum(
        jnp.dot(attended, out_weight, preferred_element_type=jnp.float32).astype(jnp.bfloat16), "tp"
    ).astype(jnp.float32)
    result = lax.dynamic_slice_in_dim(whole, lax.axis_index("tp") * columns, columns, 1).astype(
        jnp.bfloat16
    )
    return result


def solution(mesh):
    placed = (P("ctx", "tp"), P("ctx", None), P("ctx", None), P("tp", None), P())
    return jax.shard_map(
        body, mesh=mesh, in_specs=placed, out_specs=P("ctx", "tp"), check_vma=False
    )
```

profile of v0, /device:TPU:4, one launch (start us, length us, event | category | flops | bytes accessed | tf_op | source)
XLA Modules:
  0.0 654.9 jit_solution(2344125904926054323)
XLA Ops:
  6.5 0.9 copy-done
  7.5 0.6 constant_dynamic-slice_fusion.1
  8.2 1.5 constant_dynamic-slice_fusion
  9.7 1.0 copy.8
  10.9 0.9 fusion.23
  11.8 66.0 %all-gather.3.cloned.1.call-done = bf16[8192,128]{1,0:T(8,128)(2,1)} async-done(((bf16[256,128]{1,0:T(8,128)(2,1)}), bf16[8192,128]{1,0:T(8,128)(2,1)}) %all-gather.3.cloned.1.call-update) | async-done | bytes 2097168 | tf_op jit(solution)/shard_map/all_gather | solution.py:62
  77.8 66.0 %all-gather.5.cloned.1.call-done = bf16[8192,128]{1,0:T(8,128)(2,1)} async-done(((bf16[256,128]{1,0:T(8,128)(2,1)}), bf16[8192,128]{1,0:T(8,128)(2,1)}) %all-gather.5.cloned.1.call-update) | async-done | bytes 2097168 | tf_op jit(solution)/shard_map/all_gather | solution.py:63
  143.8 73.1 %while.17 = (s32[]{:T(128)}, f32[2,256]{1,0:T(2,128)S(1)}, f32[2,256]{1,0:T(2,128)S(1)}, f32[2,256,128]{2,1,0:T(8,128)S(1)}, s32[16]{0:T(128)S(1)}, /*index=5*/b...) while((s32[]{:T(128)}, f32[2,256]{1,0:T(2,128)S(1)}, ...), condition=%wide.region_6.7_spmd.clone, body=%wide.region_0.6_spmd.clone.sunk | while | flops 153822208 | bytes 4690489 | solution.py:73
  143.8 0.6 dynamic_slice.55
  145.1 1.0 fusion.37
  146.7 3.0 conditional.3
  146.7 1.2 fusion.28
  148.2 1.4 convolution_add_fusion
  149.7 0.6 dynamic_slice.55
  151.0 1.0 fusion.37
  152.6 3.0 conditional.3
  152.6 1.2 fusion.28
  154.1 1.4 convolution_add_fusion
  156.8 1.0 fusion.37
  158.4 3.0 conditional.3
  158.5 1.2 fusion.28
  160.0 1.4 convolution_add_fusion
  162.7 1.0 fusion.37
  164.3 3.0 conditional.3
  164.3 1.2 fusion.28
  165.8 1.4 convolution_add_fusion
  168.6 1.0 fusion.37
  170.2 3.0 conditional.3
  170.2 1.2 fusion.28
  171.7 1.4 convolution_add_fusion
  173.2 0.6 dynamic_slice.55
  174.4 1.0 fusion.37
  176.0 3.0 conditional.3
  176.1 1.2 fusion.28
  177.6 1.4 convolution_add_fusion
  179.0 0.6 dynamic_slice.55
  180.3 1.0 fusion.37
  181.9 3.0 conditional.3
  181.9 1.2 fusion.28
  183.4 1.4 convolution_add_fusion
  184.9 0.6 dynamic_slice.55
  186.2 1.0 fusion.37
  187.8 3.0 conditional.3
  187.8 1.2 fusion.28
  189.3 1.4 convolution_add_fusion
  190.8 0.6 dynamic_slice.55
  192.1 1.0 fusion.37
  193.6 3.0 conditional.3
  193.7 1.2 fusion.28
  195.2 1.4 convolution_add_fusion
  196.6 0.6 dynamic_slice.55
  197.9 1.0 fusion.37
  199.6 0.6 dynamic_slice.55
  200.8 1.0 fusion.37
  202.5 0.6 dynamic_slice.55
  203.7 1.0 fusion.37
  206.6 1.0 fusion.37
  209.5 1.0 fusion.37
  211.2 0.6 dynamic_slice.55
  212.4 1.0 fusion.37
  215.3 1.0 fusion.37
  217.1 5.4 convolution_convert_fusion
  222.6 424.1 %all-reduce.2.cloned.1.call-done = bf16[256,8192]{1,0:T(8,128)(2,1)} async-done(((bf16[256,8192]{1,0:T(8,128)(2,1)}), bf16[256,8192]{1,0:T(8,128)(2,1)}) %all-reduce.2.cloned.1.call-update) | async-done | bytes 4194320 | tf_op jit(solution)/shard_map/psum | solution.py:82
  646.7 1.7 convert_convert_fusion
  (96 shorter events, 6.7 us)
Async XLA Ops:
  6.5 1.0 copy-start
  6.5 71.3 %all-gather.3.cloned.1.call-start = ((), (), s32[]{:S(2)}) async-start(), calls=%async_computation | async-start | bytes 2162688 | tf_op jit(solution)/shard_map/all_gather | solution.py:62
  8.1 135.6 %all-gather.5.cloned.1.call-start = ((), (), s32[]{:S(2)}) async-start(), calls=%async_computation.1 | async-start | bytes 2162688 | tf_op jit(solution)/shard_map/all_gather | solution.py:63
  9.7 637.1 %all-reduce.2.cloned.1.call-start = ((), (), s32[]{:S(2)}) async-start(), calls=%async_computation.2 | async-start | bytes 8388608 | tf_op jit(solution)/shard_map/psum | solution.py:82
Sparse Core Ops, SparseCore 0:
  9.5 68.2 all-gather.2
  79.9 63.8 all-gather.4
  222.7 423.9 all-reduce.1
where the time goes:
time: 656 us; the launch traced here: 655 us
  waiting for transfers between devices  556 us (85%)
  matrix products  46.2 us (7%)
  loops' own time  21.4 us (3%)
  local copies, waits for them, and re-layouts  13.9 us (2%)
  between operations  13.2 us (2%)
    psum x1, waiting for transfers between devices, body(): lax.psum(jnp.dot(attended, out_weight, preferred_element_type=jnp.float32...  424 us
    all_gather x1, waiting for transfers between devices, body(): values_part = lax.all_gather(own_values, 'ctx', axis=0, tiled=True)  66 us
    all_gather x1, waiting for transfers between devices, body(): keys_part = lax.all_gather(local_keys, 'ctx', axis=0, tiled=True)  66 us
    another operation x1, loops' own time, body(): carry, unused = lax.scan(inner, carry, jnp.arange(count // stride))  20.9 us
    dot_general x16, matrix products, update(): allowed = jnp.dot(row_mask, one_hot) > 0.5  15.7 us
  transfers between devices with their start and end apart: 3, of which 3 were waited for; matrix products, arithmetic and copies ran while one was open for 1% of the time, Pallas kernels for 0%

commit v1 on v0

--- a/solution.py
+++ b/solution.py
@@ -59,7 +59,9 @@
         jnp.zeros((heads, rows, HDIM), jnp.float32),
     )
     carry = initial
-    keys_part = lax.all_gather(local_keys, "ctx", axis=0, tiled=True)
+    keys_part = jnp.concatenate(
+        lax.all_to_all(jnp.stack([local_keys] * lax.axis_size("ctx")), "ctx", 0, 0), axis=0
+    )
     values_part = lax.all_gather(own_values, "ctx", axis=0, tiled=True)
     count = keys_part.shape[0]
     stride = 512

time: 656 us -> 602 us (0.918)
  waiting for transfers between devices: 556 us -> 499 us
  starting transfers between devices: 0.09 us -> 9.7 us
  matrix products: 46.2 us -> 37.8 us
    all_gather x1 -> x0, waiting for transfers between devices: 66 us -> none  [body(): keys_part = lax.all_gather(local_keys, 'ctx', axis=0, tiled=True)]
    all_to_all x0 -> x1, starting transfers between devices: none -> 9.62 us  [body(): lax.all_to_all(jnp.stack([local_keys] * lax.axis_size('ctx')), 'ctx', 0, 0)]
    dot_general x9, matrix products: 11.1 us -> 2.91 us  [compute(): jnp.einsum('qhd,kd->hqk', query, keys_part, preferred_element_type=jnp.fl...]
  transfers between devices with their start and end apart: 3 -> 3, of which waited for: 3 -> 2; matrix products, arithmetic and copies ran while one was open for 1% -> 0% of each run, Pallas kernels for 0% -> 0%
where the time goes in v1:
time: 602 us; the launch traced here: 601 us
  waiting for transfers between devices  499 us (83%)
  matrix products  37.8 us (6%)
  loops' own time  22.5 us (4%)
  local copies, waits for them, and re-layouts  14.2 us (2%)
  between operations  13.5 us (2%)
  starting transfers between devices  9.7 us (2%)
    psum x1, waiting for transfers between devices, body(): lax.psum(jnp.dot(attended, out_weight, preferred_element_type=jnp.float32...  428 us
    all_gather x1, waiting for transfers between devices, body(): values_part = lax.all_gather(own_values, 'ctx', axis=0, tiled=True)  71.3 us
    another operation x1, loops' own time, body(): carry, unused = lax.scan(inner, carry, jnp.arange(count // stride))  22 us
    dot_general x16, matrix products, update(): allowed = jnp.dot(row_mask, one_hot) > 0.5  16.3 us
    dot_general x9, matrix products, compute(): jnp.einsum('hqk,kd->hqd', weights.astype(jnp.bfloat16), values_part, pref...  13 us
  transfers between devices with their start and end apart: 3, of which 2 were waited for; matrix products, arithmetic and copies ran while one was open for 0% of the time, Pallas kernels for 0%

profile of v1, /device:TPU:4, one launch (start us, length us, event | category | flops | bytes accessed | tf_op | source)
XLA Modules:
  0.0 601.0 jit_solution(4013968623165272818)
XLA Ops:
  6.5 0.9 copy-done
  7.5 1.8 stack.2
  9.3 9.6 %all-to-all-start = ((bf16[32,256,128]{2,1,0:T(8,128)(2,1)}), bf16[32,256,128]{2,1,0:T(8,128)(2,1)S(1)}, u32[]{:S(2)}, u32[]{:S(2)}) async-start(bf16[32,256,128]{2,1,0:T(8,128)(2,1)} %stack.2), calls=%async_computation | async-start | bytes 4194304 | tf_op jit(solution)/shard_map/all_to_all | solution.py:63
  19.0 1.5 constant_dynamic-slice_fusion
  21.0 71.3 %all-gather.2.cloned.1.call-done = bf16[8192,128]{1,0:T(8,128)(2,1)} async-done(((bf16[256,128]{1,0:T(8,128)(2,1)}), bf16[8192,128]{1,0:T(8,128)(2,1)}) %all-gather.2.cloned.1.call-update) | async-done | bytes 2097168 | tf_op jit(solution)/shard_map/all_gather | solution.py:65
  92.3 66.7 %while.17 = (s32[]{:T(128)}, f32[2,256]{1,0:T(2,128)S(1)}, f32[2,256]{1,0:T(2,128)S(1)}, f32[2,256,128]{2,1,0:T(8,128)S(1)}, s32[16]{0:T(128)S(1)}, /*index=5*/b...) while((s32[]{:T(128)}, f32[2,256]{1,0:T(2,128)S(1)}, ...), condition=%wide.region_6.7_spmd.clone, body=%wide.region_0.6_spmd.clone.sunk | while | flops 153822208 | bytes 4690489 | solution.py:75
  92.3 0.6 dynamic_slice.55
  93.6 1.0 fusion.37
  95.3 2.1 conditional.3
  95.3 0.3 fusion.28
  95.9 1.4 convolution_add_fusion
  97.4 0.6 dynamic_slice.55
  98.6 1.0 fusion.37
  100.3 2.1 conditional.3
  100.4 0.3 fusion.28
  100.9 1.4 convolution_add_fusion
  102.4 0.6 dynamic_slice.55
  103.7 1.0 fusion.37
  105.4 2.1 conditional.3
  106.0 1.4 convolution_add_fusion
  107.5 0.6 dynamic_slice.55
  108.8 1.0 fusion.37
  110.5 2.1 conditional.3
  110.5 0.3 fusion.28
  111.1 1.4 convolution_add_fusion
  112.6 0.6 dynamic_slice.55
  113.8 1.0 fusion.37
  115.5 2.1 conditional.3
  116.1 1.4 convolution_add_fusion
  117.6 0.6 dynamic_slice.55
  118.9 1.0 fusion.37
  120.6 2.1 conditional.3
  121.2 1.4 convolution_add_fusion
  122.7 0.6 dynamic_slice.55
  124.0 1.0 fusion.37
  125.7 2.1 conditional.3
  125.7 0.3 fusion.28
  126.3 1.4 convolution_add_fusion
  127.8 0.6 dynamic_slice.55
  129.0 1.0 fusion.37
  130.7 2.1 conditional.3
  131.3 1.4 convolution_add_fusion
  132.8 0.6 dynamic_slice.55
  134.1 1.0 fusion.37
  135.8 2.1 conditional.3
  135.8 0.3 fusion.28
  136.4 1.4 convolution_add_fusion
  137.9 0.6 dynamic_slice.55
  139.2 1.0 fusion.37
  140.9 0.6 dynamic_slice.55
  142.2 1.0 fusion.37
  143.9 0.6 dynamic_slice.55
  145.2 1.0 fusion.37
  146.9 0.6 dynamic_slice.55
  148.2 1.0 fusion.37
  149.9 0.6 dynamic_slice.55
  151.2 1.0 fusion.37
  153.0 0.6 dynamic_slice.55
  154.2 1.0 fusion.37
  156.0 0.6 dynamic_slice.55
  157.2 1.0 fusion.37
  159.1 5.4 convolution_convert_fusion
  164.6 427.9 %all-reduce.2.cloned.1.call-done = bf16[256,8192]{1,0:T(8,128)(2,1)} async-done(((bf16[256,8192]{1,0:T(8,128)(2,1)}), bf16[256,8192]{1,0:T(8,128)(2,1)}) %all-reduce.2.cloned.1.call-update) | async-done | bytes 4194320 | tf_op jit(solution)/shard_map/psum | solution.py:84
  592.5 1.7 convert_convert_fusion
  (100 shorter events, 4.7 us)
Async XLA Ops:
  6.5 1.0 copy-start
  6.5 14.0 %copy-start.1 = (bf16[256,256]{1,0:T(8,128)(2,1)S(1)}, bf16[256,256]{1,0:T(8,128)(2,1)}, u32[]{:S(2)}) copy-start(bf16[256,256]{1,0:T(8,128)(2,1)} %param.9) | copy-start | bytes 393220
  6.5 14.2 %copy-start.2 = (s32[64,64]{1,0:T(8,128)S(1)}, s32[64,64]{1,0:T(8,128)}, u32[]{:S(2)}) copy-start(s32[64,64]{1,0:T(8,128)} %param.13) | copy-start | bytes 49156
  9.3 83.0 %all-to-all-start = ((bf16[32,256,128]{2,1,0:T(8,128)(2,1)}), bf16[32,256,128]{2,1,0:T(8,128)(2,1)S(1)}, u32[]{:S(2)}, u32[]{:S(2)}) async-start(bf16[32,256,128]{2,1,0:T(8,128)(2,1)} %stack.2), calls=%async_computation | async-start | bytes 4194304 | tf_op jit(solution)/shard_map/all_to_all | solution.py:63
  18.9 73.3 %all-gather.2.cloned.1.call-start = ((), (), s32[]{:S(2)}) async-start(), calls=%async_computation.1 | async-start | bytes 2162688 | tf_op jit(solution)/shard_map/all_gather | solution.py:65
  20.5 572.0 %all-reduce.2.cloned.1.call-start = ((), (), s32[]{:S(2)}) async-start(), calls=%async_computation.2 | async-start | bytes 8388608 | tf_op jit(solution)/shard_map/psum | solution.py:84
Sparse Core Ops, SparseCore 0:
  21.9 70.3 all-gather.1
  164.7 427.7 all-reduce.1
